TPU v7x, 32 devices: a whole 2x2x4 slice. The times are simulated.
32 devices in a mesh: ia: 2 (over x), ja: 4 (over y, core), ka: 4 (over z).
Axes of the slice: x: 2, y: 2, z: 4, core: 2. Of those that a mesh axis runs over, the one named last changes fastest.
Arguments:
- tensor: bfloat16 [512, 512, 512], P('ia', 'ja', 'ka'), may hold values from 0 to 122880
- matrix: bfloat16 [512, 32768], P(None, ('ia', 'ja', 'ka')), may hold values from 0 to 4096000
- first_factor: bfloat16 [512, 256], P('ia'), may hold values from 0.05 to 2
- second_factor: bfloat16 [512, 256], P('ja'), may hold values from 0.05 to 2
- time_factor: bfloat16 [512, 256], P('ka'), may hold values from 0.05 to 2
- column_factor: bfloat16 [32768, 256], P(('ia', 'ja', 'ka')), may hold values from 0.05 to 2
Outputs:
- first_new: bfloat16 [512, 256], P('ia')
- second_new: bfloat16 [512, 256], P('ja')
- time_new: bfloat16 [512, 256], P('ka')
All inputs are finite; a program needn't handle non-finite values.
Results may differ from a plain program's by a relative error of at most 0.00075.
The roundings to bfloat16 on the way count: a program that leaves them out, or rounds other values in their place, can miss the bound.
Values may be sent and summed in bfloat16 or wider, within the bound.
No kernel may reach another device: no remote copies, remote signals or barrier semaphores. Data moves between devices by JAX's collectives and lax.ppermute only.
A program may use at most 128 MiB of HBM per device.

v0:
```python
import jax
import jax.numpy as jnp
from jax import lax
from jax.sharding import PartitionSpec as P


def cross_product(values):
    return jnp.dot(values.T, values, preferred_element_type=jnp.float32)


def rescale(factor, numerator, gram_total):
    widened = factor.astype(jnp.float32)
    denominator = jnp.dot(widened, gram_total, precision=lax.Precision.HIGHEST)
    return (widened * numerator / denominator).astype(jnp.bfloat16)


def on_device(tensor, matrix, first_factor, second_factor, time_factor, column_factor):
    first_rows = lax.axis_index("ia") == 0
    first_plane = lax.axis_index("ja") == 0
    first_time = lax.axis_index("ka") == 0
    gram_second = jnp.where(first_rows & first_time, cross_product(second_factor), 0.0)
    gram_time = jnp.where(first_rows & first_plane, cross_product(time_factor), 0.0)
    gram_column = cross_product(column_factor)
    gram_second, gram_time, gram_column = lax.psum(
        (gram_second, gram_time, gram_column), ("ia", "ja", "ka")
    )
    gram_total = gram_second * gram_time + gram_column
    tile_i, tile_j, tile_k = tensor.shape
    rank_size = first_factor.shape[1]
    khatri = (
        (
            second_factor.astype(jnp.float32)[:, None, :]
            * time_factor.astype(jnp.float32)[None, :, :]
        )
        .astype(jnp.bfloat16)
        .reshape(tile_j * tile_k, rank_size)
    )
    slab = jnp.dot(
        tensor.reshape(tile_i, tile_j * tile_k), khatri, preferred_element_type=jnp.float32
    )
    coupled = jnp.dot(matrix, column_factor, preferred_element_type=jnp.float32)
    offset = lax.axis_index("ia") * tile_i
    coupled = lax.psum(coupled, ("ia", "ja", "ka"))
    slab = lax.psum(slab, ("ja", "ka"))
    numerator = slab + lax.dynamic_slice_in_dim(coupled, offset, tile_i, 0)
    first_new = rescale(first_factor, numerator, gram_total)
    weighted = lax.dot_general(
        tensor, first_new, (((0,), (0,)), ((), ())), preferred_element_type=jnp.float32
    )
    plane_sum = jnp.sum(weighted * time_factor.astype(jnp.float32)[None, :, :], axis=1)
    gram_first = jnp.where(first_time, cross_product(first_new), 0.0)
    plane_sum, gram_first = lax.psum((plane_sum, gram_first), ("ia", "ka"))
    second_new = rescale(second_factor, plane_sum, gram_first * gram_time)
    time_sum = jnp.sum(weighted * second_new.astype(jnp.float32)[:, None, :], axis=0)
    gram_new = jnp.where(first_rows, cross_product(second_new), 0.0)
    time_sum, gram_new = lax.psum((time_sum, gram_new), ("ia", "ja"))
    time_new = rescale(time_factor, time_sum, gram_first * gram_new)
    return (first_new, second_new, time_new)


def solution(mesh):
    return jax.shard_map(
        on_device,
        mesh=mesh,
        in_specs=(
            P("ia", "ja", "ka"),
            P(None, ("ia", "ja", "ka")),
            P("ia", None),
            P("ja", None),
            P("ka", None),
            P(("ia", "ja", "ka"), None),
        ),
        out_specs=(P("ia", None), P("ja", None), P("ka", None)),
        check_vma=False,
    )
```

profile of v0, /device:TPU:0, one launch (start us, length us, event | category | flops | bytes accessed | tf_op | source)
XLA Modules:
  0.0 419.7 jit_solution(8857170066738423173)
XLA Ops:
  7.2 0.0 copy-start
  7.2 0.0 copy-start.4
  7.2 0.0 all-reduce.8.cloned.1.call-start
  7.2 1.0 copy.26
  8.3 0.1 copy.27
  8.4 0.0 copy-start.1
  8.4 0.0 copy-start.5
  8.4 13.1 %copy.32 = bf16[256,128,128]{0,2,1:T(8,128)(2,1)} copy(bf16[256,128,128]{2,1,0:T(8,128)(2,1)} %param.6) | data formatting | bytes 16777216 | tf_op args[0]
  21.6 0.0 copy-done.4
  21.6 0.0 copy-start.6
  21.6 0.1 copy.24
  21.7 0.1 copy.25
  21.8 6.5 %fusion.4 = f32[256,256]{0,1:T(8,128)} fusion(bf16[256,128,128]{0,2,1:T(8,128)(2,1)} %copy.32, f32[128,256]{1,0:T(8,128)S(1)} %copy.27, f32[128,256]{1,0:T(8,128)S(1)} %copy.25), kind=kOutput, calls=%fused_computation.12 | convolution fusion | flops 2155872256 | bytes 8912896 | tf_op jit(solution)/shard_map/dot_general | solution.py:38
  28.3 0.0 all-reduce.8.cloned.1.call-update
  28.3 0.0 all-reduce.10.cloned.1.call-start
  28.3 0.9 convolution_select_fusion.3
  29.3 0.0 copy-done.1
  29.3 1.0 fusion.15
  30.3 0.0 copy-done
  30.3 1.3 fusion.14
  31.6 0.0 copy-done.5
  31.6 0.9 convolution_select_fusion.2
  32.5 0.0 all-reduce.10.cloned.1.call-update
  32.5 0.0 all-reduce.12.cloned.1.call-start
  32.6 0.0 copy-done.6
  32.6 0.1 copy.23
  32.7 88.2 %all-reduce.8.cloned.1.call-done = f32[256,256]{0,1:T(8,128)} async-done(((f32[256,256]{0,1:T(8,128)}), f32[256,256]{0,1:T(8,128)}) %all-reduce.8.cloned.1.call-update) | async-done | bytes 262160 | tf_op jit(solution)/shard_map/psum | solution.py:44
  120.9 139.3 %all-reduce.10.cloned.1.call-done = (f32[256,256]{1,0:T(8,128)}, f32[256,256]{1,0:T(8,128)}, f32[256,256]{1,0:T(8,128)}, f32[512,256]{0,1:T(8,128)}) async-done(((f32[256,256]{1,0:T(8,128)}, f32[256,256]{1,0:T(8,128)}, f32[256,256]{1,0:T(8,128)}, f32[512,256]{0,1:T(8,128)}), (f32[256,256]{1,0:T(8,128)}, f32[256,256]{1,0:T(8,128)}, f32[256,256]{1,0:T(8,128)}, ...) | async-done | bytes 1310736 | tf_op jit(solution)/shard_map/psum | solution.py:24
  260.2 0.0 copy-start.2
  260.2 1.7 fusion.5
  261.9 0.9 convolution_select_fusion.1
  262.8 11.5 %multiply_reduce_fusion.1 = (f32[128,256]{1,0:T(8,128)S(1)}, f32[256,16384]{0,1}) fusion(f32[128,256]{1,0:T(8,128)S(1)} %copy.27, bf16[256,256]{0,1:T(8,128)(2,1)S(1)} %fusion.5, bf16[256,16384]{0,1:T(8,128)(2,1)} %bitcast.46), kind=kOutput, calls=%fused_computation.1 | convolution fusion | flops 2155839488 | bytes 25559040
  274.3 0.8 copy.33
  275.1 0.0 all-reduce.12.cloned.1.call-update
  275.1 0.0 all-reduce.14.cloned.1.call-start
  275.1 71.3 %all-reduce.12.cloned.1.call-done = (f32[256,256]{1,0:T(8,128)}, f32[128,256]{0,1:T(8,128)}) async-done(((f32[256,256]{1,0:T(8,128)}, f32[128,256]{0,1:T(8,128)}), (f32[256,256]{1,0:T(8,128)}, f32[128,256]{0,1:T(8,128)})) %all-reduce.12.cloned.1.call-update) | async-done | bytes 393232 | tf_op jit(solution)/shard_map/psum | solution.py:52
  346.4 0.0 copy-start.3
  346.4 0.0 copy-done.2
  346.4 1.4 fusion.9
  347.9 0.1 copy.34
  348.0 0.9 convolution_select_fusion
  348.9 7.6 %multiply_reduce_fusion = f32[128,256]{1,0:T(8,128)S(1)} fusion(f32[128,128,256]{2,1,0:T(8,128)} %bitcast.45, f32[128,256]{1,0:T(8,128)S(1)} %copy.34), kind=kLoop, calls=%fused_computation | loop fusion | flops 8355840 | bytes 17039360 | tf_op jit(solution)/shard_map/reduce_sum | solution.py:54
  356.5 0.8 copy.35
  357.3 0.0 all-reduce.14.cloned.1.call-update
  357.3 0.8 copy.36
  358.0 0.7 copy.37
  358.8 52.2 %all-reduce.14.cloned.1.call-done = (f32[256,256]{1,0:T(8,128)}, f32[128,256]{0,1:T(8,128)}) async-done(((f32[256,256]{1,0:T(8,128)}, f32[128,256]{0,1:T(8,128)}), (f32[256,256]{1,0:T(8,128)}, f32[128,256]{0,1:T(8,128)})) %all-reduce.14.cloned.1.call-update) | async-done | bytes 393232 | tf_op jit(solution)/shard_map/psum | solution.py:56
  411.0 0.0 copy-done.3
  411.0 1.4 fusion.8
  412.4 0.7 copy.38
Async XLA Ops:
  7.2 23.1 %copy-start = (bf16[512,1024]{1,0:T(8,128)(2,1)S(1)}, bf16[512,1024]{1,0:T(8,128)(2,1)}, u32[]{:S(2)}) copy-start(bf16[512,1024]{1,0:T(8,128)(2,1)} %param.7) | copy-start | bytes 3145732
  7.2 14.4 %copy-start.4 = (bf16[128,256]{1,0:T(8,128)(2,1)S(1)}, bf16[128,256]{1,0:T(8,128)(2,1)}, u32[]{:S(2)}) copy-start(bf16[128,256]{1,0:T(8,128)(2,1)} %param.9) | copy-start | bytes 196612
  7.2 113.7 %all-reduce.8.cloned.1.call-start = ((), (), s32[]{:S(2)}) async-start(), calls=%async_computation | async-start | bytes 524288 | tf_op jit(solution)/shard_map/psum | solution.py:44
  8.4 20.9 %copy-start.1 = (bf16[1024,256]{1,0:T(8,128)(2,1)S(1)}, bf16[1024,256]{1,0:T(8,128)(2,1)}, u32[]{:S(2)}) copy-start(bf16[1024,256]{1,0:T(8,128)(2,1)} %param.11) | copy-start | bytes 1572868
  8.4 23.2 %copy-start.5 = (bf16[128,256]{1,0:T(8,128)(2,1)S(1)}, bf16[128,256]{1,0:T(8,128)(2,1)}, u32[]{:S(2)}) copy-start(bf16[128,256]{1,0:T(8,128)(2,1)} %param.10) | copy-start | bytes 196612
  21.6 11.0 %copy-start.6 = (bf16[256,256]{1,0:T(8,128)(2,1)S(1)}, bf16[256,256]{1,0:T(8,128)(2,1)}, u32[]{:S(2)}) copy-start(bf16[256,256]{1,0:T(8,128)(2,1)} %param.8) | copy-start | bytes 393220
  28.3 231.9 %all-reduce.10.cloned.1.call-start = ((), (), s32[]{:S(2)}) async-start(), calls=%async_computation.1 | async-start | bytes 2621440 | tf_op jit(solution)/shard_map/psum | solution.py:24
  32.5 313.9 %all-reduce.12.cloned.1.call-start = ((), (), s32[]{:S(2)}) async-start(), calls=%async_computation.2 | async-start | bytes 786432 | tf_op jit(solution)/shard_map/psum | solution.py:52
  260.2 86.3 %copy-start.2 = (f32[256,256]{1,0:T(8,128)S(1)}, f32[256,256]{1,0:T(8,128)}, u32[]{:S(2)}) copy-start(f32[256,256]{1,0:T(8,128)} %get-tuple-element.11) | copy-start | bytes 786436
  275.1 135.9 %all-reduce.14.cloned.1.call-start = ((), (), s32[]{:S(2)}) async-start(), calls=%async_computation.3 | async-start | bytes 786432 | tf_op jit(solution)/shard_map/psum | solution.py:56
  346.4 64.6 %copy-start.3 = (f32[256,256]{1,0:T(8,128)S(1)}, f32[256,256]{1,0:T(8,128)}, u32[]{:S(2)}) copy-start(f32[256,256]{1,0:T(8,128)} %get-tuple-element.13) | copy-start | bytes 786436
Sparse Core Ops, SparseCore 0:
  28.4 92.4 all-reduce.7
  126.8 133.3 all-reduce.9
  275.2 71.1 all-reduce.11
  357.4 53.5 all-reduce.13
where the time goes:
time: 420 us
  waiting for transfers between devices  351 us (84%)
  matrix products  28.5 us (7%)
  local copies, waits for them, and re-layouts  18.5 us (4%)
  between operations  13.9 us (3%)
  other arithmetic  7.62 us (2%)
    psum x1, waiting for transfers between devices, on_device(): lax.psum((gram_second, gram_time, gram_column), ('ia', 'ja', 'ka'))  139 us
    psum x1, waiting for transfers between devices, on_device(): slab = lax.psum(slab, ('ja', 'ka'))  88.2 us
    psum x1, waiting for transfers between devices, on_device(): plane_sum, gram_first = lax.psum((plane_sum, gram_first), ('ia', 'ka'))  71.3 us
    psum x1, waiting for transfers between devices, on_device(): time_sum, gram_new = lax.psum((time_sum, gram_new), ('ia', 'ja'))  52.2 us
    unnamed x21, local copies, waits for them, and re-layouts  16.7 us
    unnamed x1, matrix products  11.5 us
  transfers between devices with their start and end apart: 4, of which 4 were waited for; matrix products, arithmetic and copies ran while one was open for 1% of the time, Pallas kernels for 0%

commit v1 on v0

--- a/solution.py
+++ b/solution.py
@@ -41,7 +41,11 @@
     coupled = jnp.dot(matrix, column_factor, preferred_element_type=jnp.float32)
     offset = lax.axis_index("ia") * tile_i
     coupled = lax.psum(coupled, ("ia", "ja", "ka"))
-    slab = lax.psum(slab, ("ja", "ka"))
+
+    def slots_test(my_data):
+        return lax.all_gather(my_data, axis_name=("ja", "ka")).sum(axis=0)
+
+    slab = slots_test(slab)
     numerator = slab + lax.dynamic_slice_in_dim(coupled, offset, tile_i, 0)
     first_new = rescale(first_factor, numerator, gram_total)
     weighted = lax.dot_general(

time: 420 us -> 345 us (0.82)
  waiting for transfers between devices: 351 us -> 269 us
    psum x1 -> x0, waiting for transfers between devices: 88.2 us -> none  [on_device(): slab = lax.psum(slab, ('ja', 'ka'))]
    all_gather x0 -> x1, waiting for transfers between devices: none -> 51.9 us  [slots_test(): return lax.all_gather(my_data, axis_name=('ja', 'ka')).sum(axis=0)]
    psum x1, waiting for transfers between devices: 139 us -> 94.7 us  [on_device(): lax.psum((gram_second, gram_time, gram_column), ('ia', 'ja', 'ka'))]
    unnamed x21 -> x22, local copies, waits for them, and re-layouts: 16.7 us -> 19.7 us
  transfers between devices with their start and end apart: 4 -> 4, of which waited for: 4 -> 4; matrix products, arithmetic and copies ran while one was open for 1% -> 3% of each run, Pallas kernels for 0% -> 0%
where the time goes in v1:
time: 345 us; the launch traced here: 344 us
  waiting for transfers between devices  269 us (78%)
  matrix products  28.3 us (8%)
  local copies, waits for them, and re-layouts  21.7 us (6%)
  between operations  15.8 us (5%)
  other arithmetic  8.68 us (3%)
    psum x1, waiting for transfers between devices, on_device(): lax.psum((gram_second, gram_time, gram_column), ('ia', 'ja', 'ka'))  94.7 us
    psum x1, waiting for transfers between devices, on_device(): plane_sum, gram_first = lax.psum((plane_sum, gram_first), ('ia', 'ka'))  70.3 us
    psum x1, waiting for transfers between devices, on_device(): time_sum, gram_new = lax.psum((time_sum, gram_new), ('ia', 'ja'))  52.4 us
    all_gather x1, waiting for transfers between devices, slots_test(): return lax.all_gather(my_data, axis_name=('ja', 'ka')).sum(axis=0)  51.9 us
    unnamed x22, local copies, waits for them, and re-layouts  19.7 us
    unnamed x1, matrix products  11.5 us
    reduce_sum x1, other arithmetic, on_device(): jnp.sum(weighted * second_new.astype(jnp.float32)[:, None, :], axis=0)  7.66 us
  transfers between devices with their start and end apart: 4, of which 4 were waited for; matrix products, arithmetic and copies ran while one was open for 3% of the time, Pallas kernels for 0%

profile of v1, /device:TPU:0, one launch (start us, length us, event | category | flops | bytes accessed | tf_op | source)
XLA Modules:
  0.0 344.1 jit_solution(9741796041934280777)
XLA Ops:
  8.0 0.0 copy-start
  8.0 0.0 all-gather.3.cloned.1.call-start
  8.1 1.0 copy.22
  9.1 0.1 copy.23
  9.2 0.0 copy-start.5
  9.2 13.1 %copy.28 = bf16[256,128,128]{0,2,1:T(8,128)(2,1)} copy(bf16[256,128,128]{2,1,0:T(8,128)(2,1)} %param.6) | data formatting | bytes 16777216 | tf_op args[0]
  22.4 0.0 copy-done.5
  22.4 0.1 copy.20
  22.5 0.1 copy.21
  22.6 0.0 copy-start.6
  22.6 0.0 copy-start.1
  22.6 6.5 %fusion.4 = f32[256,256]{0,1:T(8,128)} fusion(bf16[256,128,128]{0,2,1:T(8,128)(2,1)} %copy.28, f32[128,256]{1,0:T(8,128)S(1)} %copy.23, f32[128,256]{1,0:T(8,128)S(1)} %copy.21), kind=kOutput, calls=%fused_computation.13 | convolution fusion | flops 2155872256 | bytes 8912896 | tf_op jit(solution)/shard_map/dot_general | solution.py:38
  29.1 0.0 all-gather.3.cloned.1.call-update
  29.2 0.0 all-reduce.7.cloned.1.call-start
  29.2 0.9 convolution_select_fusion.3
  30.1 0.0 copy-done.6
  30.2 0.9 convolution_select_fusion.2
  31.1 0.0 copy-done.1
  31.1 1.0 fusion.15
  32.1 0.0 copy-done
  32.1 0.0 copy-start.7
  32.1 1.2 fusion.14
  33.4 0.0 all-reduce.7.cloned.1.call-update
  33.4 0.0 all-reduce.9.cloned.1.call-start
  33.4 51.9 %all-gather.3.cloned.1.call-done = f32[4096,256]{0,1:T(8,128)} async-done(((f32[256,256]{0,1:T(8,128)}), f32[4096,256]{0,1:T(8,128)}) %all-gather.3.cloned.1.call-update) | async-done | bytes 4194320 | tf_op jit(solution)/shard_map/all_gather | solution.py:46
  85.3 3.9 %copy.36 = f32[32,8,16,256]{3,2,1,0:T(8,128)S(1)} copy(f32[32,8,16,256]{3,1,2,0:T(8,128)} %bitcast.52) | data formatting | bytes 8388608
  89.2 1.0 bitcast_reduce_fusion
  90.3 0.1 copy.26
  90.4 94.7 %all-reduce.7.cloned.1.call-done = (f32[256,256]{1,0:T(8,128)}, f32[256,256]{1,0:T(8,128)}, f32[256,256]{1,0:T(8,128)}, f32[512,256]{1,0:T(8,128)}) async-done(((f32[256,256]{1,0:T(8,128)}, f32[256,256]{1,0:T(8,128)}, f32[256,256]{1,0:T(8,128)}, f32[512,256]{1,0:T(8,128)}), (f32[256,256]{1,0:T(8,128)}, f32[256,256]{1,0:T(8,128)}, f32[256,256]{1,0:T(8,128)}, ...) | async-done | bytes 1310736 | tf_op jit(solution)/shard_map/psum | solution.py:24
  185.1 0.0 copy-done.7
  185.1 1.5 fusion.5
  186.6 0.0 copy-start.2
  186.6 0.9 convolution_select_fusion.1
  187.6 0.0 copy-start.4
  187.6 11.5 %multiply_reduce_fusion.1 = (f32[128,256]{1,0:T(8,128)S(1)}, f32[256,16384]{0,1}) fusion(f32[128,256]{1,0:T(8,128)S(1)} %copy.23, bf16[256,16384]{0,1:T(8,128)(2,1)} %bitcast.51, bf16[256,256]{1,0:T(8,128)(2,1)S(1)} %fusion.5), kind=kOutput, calls=%fused_computation.1 | convolution fusion | flops 2155839488 | bytes 25559040
  199.1 0.0 copy-done.2
  199.1 0.8 copy.29
  199.8 0.0 all-reduce.9.cloned.1.call-update
  199.9 0.2 all-reduce.11.cloned.1.call-start
  200.1 70.3 %all-reduce.9.cloned.1.call-done = (f32[256,256]{1,0:T(8,128)}, f32[128,256]{0,1:T(8,128)}) async-done(((f32[256,256]{1,0:T(8,128)}, f32[128,256]{0,1:T(8,128)}), (f32[256,256]{1,0:T(8,128)}, f32[128,256]{0,1:T(8,128)})) %all-reduce.9.cloned.1.call-update) | async-done | bytes 393232 | tf_op jit(solution)/shard_map/psum | solution.py:56
  270.4 0.0 copy-done.4
  270.4 1.4 fusion.9
  271.8 0.1 copy.30
  271.9 0.9 convolution_select_fusion
  272.9 0.0 copy-start.3
  272.9 7.7 %multiply_reduce_fusion = f32[128,256]{1,0:T(8,128)S(1)} fusion(f32[128,128,256]{2,1,0:T(8,128)} %bitcast.50, f32[128,256]{1,0:T(8,128)S(1)} %copy.30), kind=kLoop, calls=%fused_computation | loop fusion | flops 8355840 | bytes 17039360 | tf_op jit(solution)/shard_map/reduce_sum | solution.py:58
  280.5 0.8 copy.31
  281.3 0.0 all-reduce.11.cloned.1.call-update
  281.3 0.7 copy.32
  282.0 52.4 %all-reduce.11.cloned.1.call-done = (f32[256,256]{1,0:T(8,128)}, f32[128,256]{0,1:T(8,128)}) async-done(((f32[256,256]{1,0:T(8,128)}, f32[128,256]{0,1:T(8,128)}), (f32[256,256]{1,0:T(8,128)}, f32[128,256]{0,1:T(8,128)})) %all-reduce.11.cloned.1.call-update) | async-done | bytes 393232 | tf_op jit(solution)/shard_map/psum | solution.py:60
  334.4 0.0 copy-done.3
  334.4 1.4 fusion.8
  335.8 0.7 copy.33
Async XLA Ops:
  8.0 24.1 %copy-start = (bf16[512,1024]{1,0:T(8,128)(2,1)S(1)}, bf16[512,1024]{1,0:T(8,128)(2,1)}, u32[]{:S(2)}) copy-start(bf16[512,1024]{1,0:T(8,128)(2,1)} %param.7) | copy-start | bytes 3145732
  8.0 77.3 %all-gather.3.cloned.1.call-start = ((), (), s32[]{:S(2)}) async-start(), calls=%async_computation | async-start | bytes 4456448 | tf_op jit(solution)/shard_map/all_gather | solution.py:46
  9.2 13.2 %copy-start.5 = (bf16[128,256]{1,0:T(8,128)(2,1)S(1)}, bf16[128,256]{1,0:T(8,128)(2,1)}, u32[]{:S(2)}) copy-start(bf16[128,256]{1,0:T(8,128)(2,1)} %param.9) | copy-start | bytes 196612
  22.6 7.6 %copy-start.6 = (bf16[128,256]{1,0:T(8,128)(2,1)S(1)}, bf16[128,256]{1,0:T(8,128)(2,1)}, u32[]{:S(2)}) copy-start(bf16[128,256]{1,0:T(8,128)(2,1)} %param.10) | copy-start | bytes 196612
  22.6 8.5 %copy-start.1 = (bf16[1024,256]{1,0:T(8,128)(2,1)S(1)}, bf16[1024,256]{1,0:T(8,128)(2,1)}, u32[]{:S(2)}) copy-start(bf16[1024,256]{1,0:T(8,128)(2,1)} %param.11) | copy-start | bytes 1572868
  29.2 155.9 %all-reduce.7.cloned.1.call-start = ((), (), s32[]{:S(2)}) async-start(), calls=%async_computation.1 | async-start | bytes 2621440 | tf_op jit(solution)/shard_map/psum | solution.py:24
  32.1 153.0 %copy-start.7 = (bf16[256,256]{1,0:T(8,128)(2,1)S(1)}, bf16[256,256]{1,0:T(8,128)(2,1)}, u32[]{:S(2)}) copy-start(bf16[256,256]{1,0:T(8,128)(2,1)} %param.8) | copy-start | bytes 393220
  33.4 237.1 %all-reduce.9.cloned.1.call-start = ((), (), s32[]{:S(2)}) async-start(), calls=%async_computation.2 | async-start | bytes 786432 | tf_op jit(solution)/shard_map/psum | solution.py:56
  186.6 12.5 %copy-start.2 = (bf16[256,256]{1,0:T(8,128)(2,1)}, bf16[256,256]{1,0:T(8,128)(2,1)S(1)}, u32[]{:S(2)}) copy-start(bf16[256,256]{1,0:T(8,128)(2,1)S(1)} %fusion.5) | copy-start | bytes 393220
  187.6 82.9 %copy-start.4 = (f32[256,256]{1,0:T(8,128)S(1)}, f32[256,256]{1,0:T(8,128)}, u32[]{:S(2)}) copy-start(f32[256,256]{1,0:T(8,128)} %get-tuple-element.11) | copy-start | bytes 786436
  199.9 134.5 %all-reduce.11.cloned.1.call-start = ((), (), s32[]{:S(2)}) async-start(), calls=%async_computation.3 | async-start | bytes 786432 | tf_op jit(solution)/shard_map/psum | solution.py:60
  272.9 61.6 %copy-start.3 = (f32[256,256]{1,0:T(8,128)S(1)}, f32[256,256]{1,0:T(8,128)}, u32[]{:S(2)}) copy-start(f32[256,256]{1,0:T(8,128)} %get-tuple-element.13) | copy-start | bytes 786436
Sparse Core Ops, SparseCore 0:
  29.3 55.9 all-gather.2
Sparse Core Ops, SparseCore 1:
  35.5 149.5 all-reduce.6
  199.9 70.4 all-reduce.8
  281.4 53.0 all-reduce.10
